TPU v7x, 32 devices: a whole 2x2x4 slice. The times are simulated.
32 devices in a mesh: dp: 16 (over z, x, core), tp: 2 (over y).
Axes of the slice: x: 2, y: 2, z: 4, core: 2. Of those that a mesh axis runs over, the one named last changes fastest.
Arguments:
- layer_in: bfloat16 [16384, 768], P(('dp', 'tp')), may hold values from -6 to 6
- lengths: int32 [128, 17], P('dp'), may hold values from 0 to 77, as said below
- attn_gain: float32 [768], replicated, may hold values from 0.25 to 1.75
- attn_shift: float32 [768], replicated, may hold values from -2 to 2
- qkv_weight: bfloat16 [768, 3, 768], P(None, None, 'tp'), may hold values from -0.21875 to 0.21875
- qv_bias: float32 [2, 768], P(None, 'tp'), may hold values from -3 to 3
- out_weight: bfloat16 [768, 768], P('tp'), may hold values from -0.875 to 0.875
- out_bias: float32 [768], replicated, may hold values from -2 to 2
- mlp_gain: float32 [768], replicated, may hold values from 0.25 to 1.75
- mlp_shift: float32 [768], replicated, may hold values from -2 to 2
- up_weight: bfloat16 [768, 3072], P(None, 'tp'), may hold values from -0.21875 to 0.21875
- up_bias: float32 [3072], P('tp'), may hold values from -3 to 3
- down_weight: bfloat16 [3072, 768], P('tp'), may hold values from -0.15625 to 0.15625
- down_bias: float32 [768], replicated, may hold values from -2 to 2
- cotangent: bfloat16 [16384, 768], P(('dp', 'tp')), may hold values from -6 to 6
Outputs:
- layer_out: bfloat16 [16384, 768], P(('dp', 'tp'))
- in_grad: bfloat16 [16384, 768], P(('dp', 'tp'))
- attn_gain_grad: float32 [768], replicated
- attn_shift_grad: float32 [768], replicated
- qkv_weight_grad: float32 [768, 3, 768], P(None, None, 'tp')
- qv_bias_grad: float32 [2, 768], P(None, 'tp')
- out_weight_grad: float32 [768, 768], P('tp')
- out_bias_grad: float32 [768], replicated
- mlp_gain_grad: float32 [768], replicated
- mlp_shift_grad: float32 [768], replicated
- up_weight_grad: float32 [768, 3072], P(None, 'tp')
- up_bias_grad: float32 [3072], P('tp')
- down_weight_grad: float32 [3072, 768], P('tp')
- down_bias_grad: float32 [768], replicated
Inputs may be any that keep to these rules, and one draw needn't show every extreme that they name: Row r's captions take lengths[r, 0], lengths[r, 1], ... tokens in order from slot 0; each entry is 0 or between 8 and 77; after a 0 all entries of the row are 0; a row's entries sum to at most 128, and its slots from that sum on are padding.
All inputs are finite; a program needn't handle non-finite values.
Results may differ from a plain program's by a relative error of at most 0.017.
Values may be sent and summed in bfloat16 or wider, within the bound.
No kernel may reach another device: no remote copies, remote signals or barrier semaphores. Data moves between devices by JAX's collectives and lax.ppermute only.
A program may use at most 128 MiB of HBM per device.

v0:
```python
from functools import partial
import math
import jax
import jax.numpy as jnp
from jax import lax
from jax.sharding import PartitionSpec as P

HEAD = 64
SEQ = 128
norm_epsilon = 1e-05


def layer_norm(values, gain, shift):
    center = values - jnp.mean(values, axis=-1, keepdims=True)
    spread = jnp.mean(center * center, axis=-1, keepdims=True)
    return center * lax.rsqrt(spread + norm_epsilon) * gain + shift


def segment_masks(lengths):
    seg_ends = jnp.cumsum(lengths, axis=1)
    places = jnp.arange(SEQ, dtype=jnp.int32)
    segment = jnp.sum((seg_ends[:, None, :] <= places[None, :, None]).astype(jnp.int32), axis=2)
    tok_valid = places[None, :] < seg_ends[:, -1:]
    causal = places[None, :] <= places[:, None]
    self_pair = places[None, :] == places[:, None]
    same_seg = segment[:, :, None] == segment[:, None, :]
    allowed = same_seg & causal[None] & (tok_valid[:, None, :] | self_pair[None])
    return (allowed, tok_valid)


def on_device(
    layer_in,
    lengths,
    attn_gain,
    attn_shift,
    qkv_weight,
    qv_bias,
    out_weight,
    out_bias,
    mlp_gain,
    mlp_shift,
    up_weight,
    up_bias,
    down_weight,
    down_bias,
    cotangent,
):
    model_width = layer_in.shape[1]
    local_width = qkv_weight.shape[2]
    head_count = local_width // HEAD
    row_count = lengths.shape[0]
    tok_count = row_count * SEQ
    score_scale = 1.0 / math.sqrt(HEAD)
    allowed, tok_valid = segment_masks(lengths)
    valid_col = tok_valid.astype(jnp.float32)[:, :, None, None]
    valid_low = valid_col.astype(jnp.bfloat16)
    resid_in = layer_in.astype(jnp.float32)
    normed_attn = layer_norm(resid_in, attn_gain, attn_shift).astype(jnp.bfloat16)
    gathered_attn = lax.all_gather(normed_attn, "tp", axis=0, tiled=True)
    flat_qkv = qkv_weight.reshape(model_width, 3 * local_width)
    projected = jnp.dot(gathered_attn, flat_qkv, preferred_element_type=jnp.float32)
    queries = (projected[:, :local_width] + qv_bias[0]).astype(jnp.bfloat16)
    key_rows = projected[:, local_width : 2 * local_width].astype(jnp.bfloat16)
    value_rows = (projected[:, 2 * local_width :] + qv_bias[1]).astype(jnp.bfloat16)
    query_heads = queries.reshape(row_count, SEQ, head_count, HEAD)
    key_heads = key_rows.reshape(row_count, SEQ, head_count, HEAD)
    value_heads = value_rows.reshape(row_count, SEQ, head_count, HEAD)

    def scores_of():
        raw_scores = jnp.einsum(
            "rqhd,rkhd->rhqk", query_heads, key_heads, preferred_element_type=jnp.float32
        )
        return jnp.where(allowed[:, None], raw_scores * score_scale, -1e30)

    masked = scores_of()
    row_max = jnp.max(masked, axis=-1, keepdims=True)
    exp_scores = jnp.exp(masked - row_max)
    row_total = jnp.sum(exp_scores, axis=-1, keepdims=True)
    log_total = row_max + jnp.log(row_total)
    attn_probs = exp_scores / row_total
    probs_low = attn_probs.astype(jnp.bfloat16)
    attended = (
        jnp.einsum("rhqk,rkhd->rqhd", probs_low, value_heads, preferred_element_type=jnp.float32)
        * valid_col
    )
    attended_low = attended.reshape(tok_count, local_width).astype(jnp.bfloat16)
    row_piece = attended_low
    attn_sum = lax.psum_scatter(
        jnp.dot(row_piece, out_weight, preferred_element_type=jnp.float32).astype(jnp.bfloat16),
        "tp",
        scatter_dimension=0,
        tiled=True,
    ).astype(jnp.float32)
    resid_mid = resid_in + attn_sum + out_bias
    normed_mlp = layer_norm(resid_mid, mlp_gain, mlp_shift).astype(jnp.bfloat16)
    gathered_mlp = lax.all_gather(normed_mlp, "tp", axis=0, tiled=True)
    pre_act = jnp.dot(gathered_mlp, up_weight, preferred_element_type=jnp.float32) + up_bias
    activated = jax.nn.gelu(pre_act, approximate=False).astype(jnp.bfloat16)
    row_piece = activated
    mlp_sum = lax.psum_scatter(
        jnp.dot(row_piece, down_weight, preferred_element_type=jnp.float32).astype(jnp.bfloat16),
        "tp",
        scatter_dimension=0,
        tiled=True,
    ).astype(jnp.float32)
    layer_out = (resid_mid + mlp_sum + down_bias).astype(jnp.bfloat16)
    out_grad = cotangent.astype(jnp.float32)
    grad_rows = lax.all_gather(cotangent, "tp", axis=0, tiled=True)
    down_weight_grad = jnp.einsum(
        "tf,td->fd", activated, grad_rows, preferred_element_type=jnp.float32
    )
    act_grad = jnp.einsum("td,fd->tf", grad_rows, down_weight, preferred_element_type=jnp.float32)
    gelu_value, gelu_back = jax.vjp(partial(jax.nn.gelu, approximate=False), pre_act)
    pre_grad = gelu_back(act_grad)[0].astype(jnp.bfloat16)
    up_bias_grad = jnp.sum(pre_grad.astype(jnp.float32), axis=0)
    up_weight_grad = jnp.einsum(
        "td,tf->df", gathered_mlp, pre_grad, preferred_element_type=jnp.float32
    )
    row_piece = pre_grad
    normed_mlp_grad = lax.psum_scatter(
        jnp.einsum("tf,df->td", row_piece, up_weight, preferred_element_type=jnp.float32).astype(
            jnp.bfloat16
        ),
        "tp",
        scatter_dimension=0,
        tiled=True,
    ).astype(jnp.float32)
    norm_value, mlp_norm_back = jax.vjp(layer_norm, resid_mid, mlp_gain, mlp_shift)
    mid_part, mlp_gain_grad, mlp_shift_grad = mlp_norm_back(normed_mlp_grad)
    mid_grad = out_grad + mid_part
    down_bias_grad = jnp.sum(out_grad, axis=0)
    out_bias_grad = jnp.sum(mid_grad, axis=0)
    mid_low = mid_grad.astype(jnp.bfloat16)
    mid_rows = lax.all_gather(mid_low, "tp", axis=0, tiled=True)
    out_weight_grad = jnp.einsum(
        "te,td->ed", attended_low, mid_rows, preferred_element_type=jnp.float32
    )
    attended_grad = jnp.einsum(
        "td,ed->te", mid_rows, out_weight, preferred_element_type=jnp.float32
    )
    attended_grad = (
        attended_grad.astype(jnp.bfloat16).reshape(row_count, SEQ, head_count, HEAD) * valid_low
    )
    back_probs = jnp.exp(scores_of() - log_total)
    back_low = back_probs.astype(jnp.bfloat16)
    value_grad = jnp.einsum(
        "rhqk,rqhd->rkhd", back_low, attended_grad, preferred_element_type=jnp.float32
    )
    prob_grad = jnp.einsum(
        "rqhd,rkhd->rhqk", attended_grad, value_heads, preferred_element_type=jnp.float32
    )
    row_inner = jnp.sum(back_probs * prob_grad, axis=-1, keepdims=True)
    score_grad = (back_probs * (prob_grad - row_inner)).astype(jnp.bfloat16)
    query_grad = (
        jnp.einsum("rhqk,rkhd->rqhd", score_grad, key_heads, preferred_element_type=jnp.float32)
        * score_scale
    )
    key_grad = (
        jnp.einsum("rhqk,rqhd->rkhd", score_grad, query_heads, preferred_element_type=jnp.float32)
        * score_scale
    )
    query_low = query_grad.reshape(tok_count, local_width).astype(jnp.bfloat16)
    key_low = key_grad.reshape(tok_count, local_width).astype(jnp.bfloat16)
    value_low = value_grad.reshape(tok_count, local_width).astype(jnp.bfloat16)
    qkv_grad = jnp.concatenate([query_low, key_low, value_low], axis=1)
    qv_bias_grad = jnp.stack(
        [
            jnp.sum(query_low.astype(jnp.float32), axis=0),
            jnp.sum(value_low.astype(jnp.float32), axis=0),
        ]
    )
    qkv_weight_grad = jnp.einsum(
        "td,te->de", gathered_attn, qkv_grad, preferred_element_type=jnp.float32
    )
    qkv_weight_grad = qkv_weight_grad.reshape(model_width, 3, local_width)
    row_piece = qkv_grad
    normed_attn_grad = lax.psum_scatter(
        jnp.einsum("te,de->td", row_piece, flat_qkv, preferred_element_type=jnp.float32).astype(
            jnp.bfloat16
        ),
        "tp",
        scatter_dimension=0,
        tiled=True,
    ).astype(jnp.float32)
    attn_norm_value, attn_norm_back = jax.vjp(layer_norm, resid_in, attn_gain, attn_shift)
    in_part, attn_gain_grad, attn_shift_grad = attn_norm_back(normed_attn_grad)
    in_grad = (mid_grad + in_part).astype(jnp.bfloat16)
    (
        qkv_weight_grad,
        qv_bias_grad,
        out_weight_grad,
        up_weight_grad,
        up_bias_grad,
        down_weight_grad,
    ) = lax.psum(
        (
            qkv_weight_grad,
            qv_bias_grad,
            out_weight_grad,
            up_weight_grad,
            up_bias_grad,
            down_weight_grad,
        ),
        "dp",
    )
    (
        attn_gain_grad,
        attn_shift_grad,
        out_bias_grad,
        mlp_gain_grad,
        mlp_shift_grad,
        down_bias_grad,
    ) = lax.psum(
        (
            attn_gain_grad,
            attn_shift_grad,
            out_bias_grad,
            mlp_gain_grad,
            mlp_shift_grad,
            down_bias_grad,
        ),
        ("dp", "tp"),
    )
    return (
        layer_out,
        in_grad,
        attn_gain_grad,
        attn_shift_grad,
        qkv_weight_grad,
        qv_bias_grad,
        out_weight_grad,
        out_bias_grad,
        mlp_gain_grad,
        mlp_shift_grad,
        up_weight_grad,
        up_bias_grad,
        down_weight_grad,
        down_bias_grad,
    )


def solution(mesh):
    in_specs = (
        P(("dp", "tp"), None),
        P("dp", None),
        P(),
        P(),
        P(None, None, "tp"),
        P(None, "tp"),
        P("tp", None),
        P(),
        P(),
        P(),
        P(None, "tp"),
        P("tp"),
        P("tp", None),
        P(),
        P(("dp", "tp"), None),
    )
    out_specs = (
        P(("dp", "tp"), None),
        P(("dp", "tp"), None),
        P(),
        P(),
        P(None, None, "tp"),
        P(None, "tp"),
        P("tp", None),
        P(),
        P(),
        P(),
        P(None, "tp"),
        P("tp"),
        P("tp", None),
        P(),
    )
    return jax.shard_map(
        on_device, mesh=mesh, in_specs=in_specs, out_specs=out_specs, check_vma=False
    )
```

profile of v0, /device:TPU:0, one launch (start us, length us, event | category | flops | bytes accessed | tf_op | source)
XLA Modules:
  0.0 599.3 jit_solution(7558251490497962483)
XLA Ops:
  13.0 3.8 copy.64
  17.5 25.2 %all-gather.5.cloned.1.call-done = bf16[1024,768]{1,0:T(8,128)(2,1)} async-done(((bf16[512,768]{1,0:T(8,128)(2,1)}), bf16[1024,768]{1,0:T(8,128)(2,1)}) %all-gather.5.cloned.1.call-update) | async-done | bytes 1572880 | tf_op jit(solution)/shard_map/all_gather | solution.py:59
  42.7 4.2 fusion.59
  66.3 26.2 %reduce-scatter.5.cloned.1.call-done = bf16[512,768]{1,0:T(8,128)(2,1)} async-done(((bf16[1024,768]{1,0:T(8,128)(2,1)}), bf16[512,768]{1,0:T(8,128)(2,1)}) %reduce-scatter.5.cloned.1.call-update) | async-done | bytes 786448 | tf_op jit(solution)/shard_map/reduce_scatter | solution.py:88
  98.1 26.3 %all-gather.7.cloned.1.call-done = bf16[1024,768]{1,0:T(8,128)(2,1)} async-done(((bf16[512,768]{1,0:T(8,128)(2,1)}), bf16[1024,768]{1,0:T(8,128)(2,1)}) %all-gather.7.cloned.1.call-update) | async-done | bytes 1572880 | tf_op jit(solution)/shard_map/all_gather | solution.py:96
  124.4 7.4 %fusion.60 = f32[1024,1536]{1,0:T(8,128)} fusion(bf16[1024,768]{1,0:T(8,128)(2,1)} %all-gather.7.cloned.1.call-done, bf16[768,1536]{1,0:T(8,128)(2,1)} %param.25), kind=kOutput, calls=%fused_computation.128 | convolution fusion | flops 2415919104 | bytes 10223616 | tf_op jit(solution)/shard_map/dot_general | solution.py:97
  131.8 21.3 %all-gather.9.cloned.1.call-done = bf16[1024,768]{1,0:T(8,128)(2,1)} async-done(((bf16[512,768]{1,0:T(8,128)(2,1)}), bf16[1024,768]{1,0:T(8,128)(2,1)}) %all-gather.9.cloned.1.call-update) | async-done | bytes 1572880 | tf_op jit(solution)/shard_map/all_gather | solution.py:108
  153.1 19.3 %convert_reduce_fusion = (f32[1536]{0:T(1024)S(1)}, bf16[1024,1536]{1,0:T(8,128)(2,1)S(1)}, f32[1024,1536]{1,0:T(8,128)}) fusion(f32[1024,1536]{1,0:T(8,128)} %fusion.60, f32[1536]{0:T(1024)S(1)} %copy-done.25, bf16[1024,768]{1,0:T(8,128)(2,1)} %all-gather.9.cloned.1.call-done, bf16[1536,768]{1,0:T(8,128)(2,1)S(1)} %copy-done), kind=kOutput, calls=%fused_computation.2 | convolution fusion | flops 2533882368 | bytes 19673088 | tf_op jit(solution)/shard_map/td,fd->tf/dot_general | solution.py:112
  174.1 3.8 convolution_convert_fusion.2
  177.9 6.2 %multiply_convert_fusion = bf16[1024,1536]{1,0:T(8,128)(2,1)S(1)} fusion(f32[1024,1536]{1,0:T(8,128)} %get-tuple-element.66, f32[1024,1536]{1,0:T(8,128)} %fusion.60, f32[1536]{0:T(1024)S(1)} %copy-done.25), kind=kLoop, calls=%fused_computation.4 | loop fusion | flops 6291456 | bytes 15734784 | tf_op jit(solution)/shard_map/convert_element_type | solution.py:98
  185.8 3.7 convolution_convert_fusion.3
  189.6 14.6 %reduce-scatter.9.cloned.1.call-done = bf16[512,768]{1,0:T(8,128)(2,1)} async-done(((bf16[1024,768]{1,0:T(8,128)(2,1)}), bf16[512,768]{1,0:T(8,128)(2,1)}) %reduce-scatter.9.cloned.1.call-update) | async-done | bytes 786448 | tf_op jit(solution)/shard_map/reduce_scatter | solution.py:120
  207.5 24.8 %reduce-scatter.7.cloned.1.call-done = bf16[512,768]{1,0:T(8,128)(2,1)} async-done(((bf16[1024,768]{1,0:T(8,128)(2,1)}), bf16[512,768]{1,0:T(8,128)(2,1)}) %reduce-scatter.7.cloned.1.call-update) | async-done | bytes 786448 | tf_op jit(solution)/shard_map/reduce_scatter | solution.py:100
  232.3 3.7 fusion.57
  238.5 27.1 %all-gather.11.cloned.1.call-done = bf16[1024,768]{1,0:T(8,128)(2,1)} async-done(((bf16[512,768]{1,0:T(8,128)(2,1)}), bf16[1024,768]{1,0:T(8,128)(2,1)}) %all-gather.11.cloned.1.call-update) | async-done | bytes 1572880 | tf_op jit(solution)/shard_map/all_gather | solution.py:134
  282.0 3.5 convolution_convert_fusion.1
  285.9 7.4 %fusion.62 = f32[1536,768]{1,0:T(8,128)} fusion(bf16[1024,1536]{1,0:T(8,128)(2,1)} %copy-done.8, bf16[1024,768]{1,0:T(8,128)(2,1)} %all-gather.9.cloned.1.call-done), kind=kOutput, calls=%fused_computation.130 | convolution fusion | flops 2415919104 | bytes 9437184 | tf_op jit(solution)/shard_map/tf,td->fd/dot_general | solution.py:109
  293.3 4.4 fusion.61
  300.2 3.8 fusion.63
  304.2 63.9 %all-reduce.1 = (f32[2,384]{1,0:T(2,128)}, f32[1536]{0:T(1024)}) all-reduce(f32[2,384]{1,0:T(2,128)S(1)} %pad_maximum_fusion, f32[1536]{0:T(1024)S(1)} %get-tuple-element.64), channel_id=1, replica_groups=mesh['dp'=16,'tp'=2] {'dp'}, use_global_device_ids=true, to_apply=%region_24.25 | all-reduce | flops 2304 | bytes 18432 | tf_op jit(solution)/shard_map/psum | solution.py:195
  372.0 39.3 %all-reduce = (f32[768]{0:T(1024)}, f32[768]{0:T(1024)}, f32[768]{0:T(1024)}, f32[768]{0:T(1024)}, f32[768]{0:T(1024)}, /*index=5*/f32[768]{0:T(1024)}) all-reduce(f32[768]{0:T(1024)S(1)} %get-tuple-element.44, f32[768]{0:T(1024)S(1)} %get-tuple-element.48, ...), channel_id=1, replica_groups=mesh['dp'=16,'tp'=2] {'dp','tp'}, use_global_device_ids=true, to_apply=%region_18.19 | all-reduce | flops 4608 | bytes 36864 | tf_op jit(solution)/shard_map/psum | solution.py:213
  414.4 163.4 %all-reduce.5.cloned.1.call-done = (f32[768,3,384]{0,2,1:T(8,128)}, f32[384,768]{1,0:T(8,128)}, f32[768,1536]{1,0:T(8,128)}, f32[1536,768]{1,0:T(8,128)}) async-done(((f32[768,3,384]{0,2,1:T(8,128)}, f32[384,768]{1,0:T(8,128)}, f32[768,1536]{1,0:T(8,128)}, f32[1536,768]{1,0:T(8,128)}), (f32[768,3,384]{0,2,1:T(8,128)}, f32[384,768]{1,0:T(8,128)}, f32[768,1536]{1,0:T(8,128)}, ...) | async-done | bytes 14155792 | tf_op jit(solution)/shard_map/psum | solution.py:195
  577.8 5.2 copy.87
  585.4 4.9 copy.147
  (155 shorter events, 71.5 us)
Async XLA Ops:
  7.2 145.9 %copy-start = (bf16[1536,768]{1,0:T(8,128)(2,1)S(1)}, bf16[1536,768]{1,0:T(8,128)(2,1)}, u32[]{:S(2)}) copy-start(bf16[1536,768]{1,0:T(8,128)(2,1)} %param.27) | copy-start | bytes 7077892
  7.2 5.5 copy-start.27
  7.2 35.5 %all-gather.5.cloned.1.call-start = ((), (), s32[]{:S(2)}) async-start(), calls=%async_computation.4 | async-start | bytes 2359296 | tf_op jit(solution)/shard_map/all_gather | solution.py:59
  12.6 79.8 %reduce-scatter.5.cloned.1.call-start = ((), (), s32[]{:S(2)}) async-start(), calls=%async_computation.5 | async-start | bytes 2359296 | tf_op jit(solution)/shard_map/reduce_scatter | solution.py:88
  64.0 28.4 %copy-start.1 = (bf16[512,768]{1,0:T(8,128)(2,1)S(1)}, bf16[512,768]{1,0:T(8,128)(2,1)}, u32[]{:S(2)}) copy-start(bf16[512,768]{1,0:T(8,128)(2,1)} %param.15) | copy-start | bytes 2359300
  64.0 28.4 %copy-start.22 = (f32[768]{0:T(1024)S(1)}, f32[768]{0:T(1024)}, u32[]{:S(2)}) copy-start(f32[768]{0:T(1024)} %param.22) | copy-start | bytes 9220
  66.2 29.4 %copy-start.24 = (f32[768]{0:T(1024)S(1)}, f32[768]{0:T(1024)}, u32[]{:S(2)}) copy-start(f32[768]{0:T(1024)} %param.23) | copy-start | bytes 9220
  66.2 29.4 %copy-start.26 = (f32[768]{0:T(1024)S(1)}, f32[768]{0:T(1024)}, u32[]{:S(2)}) copy-start(f32[768]{0:T(1024)} %param.24) | copy-start | bytes 9220
  66.2 58.1 %all-gather.7.cloned.1.call-start = ((), (), s32[]{:S(2)}) async-start(), calls=%async_computation.6 | async-start | bytes 2359296 | tf_op jit(solution)/shard_map/all_gather | solution.py:96
  97.0 56.1 %all-gather.9.cloned.1.call-start = ((), (), s32[]{:S(2)}) async-start(), calls=%async_computation.8 | async-start | bytes 2359296 | tf_op jit(solution)/shard_map/all_gather | solution.py:108
  97.6 55.5 %copy-start.25 = (f32[1536]{0:T(1024)S(1)}, f32[1536]{0:T(1024)}, u32[]{:S(2)}) copy-start(f32[1536]{0:T(1024)} %param.26) | copy-start | bytes 18436
  97.6 106.5 %reduce-scatter.9.cloned.1.call-start = ((), (), s32[]{:S(2)}) async-start(), calls=%async_computation.9 | async-start | bytes 2359296 | tf_op jit(solution)/shard_map/reduce_scatter | solution.py:120
  153.1 21.0 %copy-start.30 = (bf16[768,1536]{1,0:T(8,128)(2,1)S(1)}, bf16[768,1536]{1,0:T(8,128)(2,1)}, u32[]{:S(2)}) copy-start(bf16[768,1536]{1,0:T(8,128)(2,1)} %param.25) | copy-start | bytes 7077892
  177.9 54.4 %reduce-scatter.7.cloned.1.call-start = ((), (), s32[]{:S(2)}) async-start(), calls=%async_computation.7 | async-start | bytes 2359296 | tf_op jit(solution)/shard_map/reduce_scatter | solution.py:100
  189.5 42.8 %copy-start.28 = (f32[768]{0:T(1024)S(1)}, f32[768]{0:T(1024)}, u32[]{:S(2)}) copy-start(f32[768]{0:T(1024)} %param.28) | copy-start | bytes 9220
  189.5 76.1 %all-gather.11.cloned.1.call-start = ((), (), s32[]{:S(2)}) async-start(), calls=%async_computation.10 | async-start | bytes 2359296 | tf_op jit(solution)/shard_map/all_gather | solution.py:134
  238.2 129.8 %reduce-scatter.11.cloned.1.call-start = ((), (), s32[]{:S(2)}) async-start(), calls=%async_computation.11 | async-start | bytes 2359296 | tf_op jit(solution)/shard_map/reduce_scatter | solution.py:177
  285.6 292.2 %all-reduce.5.cloned.1.call-start = ((), (), s32[]{:S(2)}) async-start(), calls=%async_computation.12 | async-start | bytes 28311552 | tf_op jit(solution)/shard_map/psum | solution.py:195
  285.9 7.4 %copy-start.13 = (bf16[1024,1536]{1,0:T(8,128)(2,1)S(1)}, bf16[1024,1536]{1,0:T(8,128)(2,1)}, u32[]{:S(2)}) copy-start(bf16[1024,1536]{1,0:T(8,128)(2,1)} %copy-done.12) | copy-start | bytes 9437188
  285.9 7.4 %copy-start.17 = (bf16[1024,768]{1,0:T(8,128)(2,1)S(1)}, bf16[1024,768]{1,0:T(8,128)(2,1)}, u32[]{:S(2)}) copy-start(bf16[1024,768]{1,0:T(8,128)(2,1)} %all-gather.7.cloned.1.call-done) | copy-start | bytes 4718596
  293.2 4.4 copy-start.19
  304.0 64.1 %copy-start.23 = (f32[768]{0:T(1024)S(1)}, f32[768]{0:T(1024)}, u32[]{:S(2)}) copy-start(f32[768]{0:T(1024)} %param.17) | copy-start | bytes 9220
  582.9 7.4 %slice-start = ((s8[4718592]{0:T(1024)(128)(4,1)}), s8[4194304]{0:T(1024)(128)(4,1)S(1)}, s32[]{:S(2)}) async-start(s8[4718592]{0:T(1024)(128)(4,1)} %bitcast.79), calls=%async_computation.13 | async-start | bytes 8388608
  585.4 4.9 slice-start.1
  (21 other events, 43.7 us)
Sparse Core Ops, SparseCore 0:
  12.8 29.8 all-gather.4
  66.3 26.0 reduce-scatter.4
  97.1 27.2 all-gather.6
  125.8 27.2 all-gather.8
  178.0 26.0 reduce-scatter.8
  206.2 26.0 reduce-scatter.6
  238.4 27.2 all-gather.10
  285.7 26.0 reduce-scatter.10
  317.5 260.1 all-reduce.4
where the time goes:
time: 608 us; the launch traced here: 599 us
  waiting for transfers between devices  329 us (54%)
  blocking collectives  103 us (17%)
  matrix products  71.8 us (12%)
  local copies, waits for them, and re-layouts  44.1 us (7%)
  other arithmetic  35 us (6%)
  between operations  14.5 us (2%)
    psum x1, waiting for transfers between devices, on_device(): lax.psum((qkv_weight_grad, qv_bias_grad, out_weight_grad, up_weight_grad,...  163 us
    psum x1, blocking collectives, on_device(): lax.psum((qkv_weight_grad, qv_bias_grad, out_weight_grad, up_weight_grad,...  63.9 us
    psum x1, blocking collectives, on_device(): lax.psum((attn_gain_grad, attn_shift_grad, out_bias_grad, mlp_gain_grad,...  39.3 us
    unnamed x83, local copies, waits for them, and re-layouts  34.2 us
    all_gather x1, waiting for transfers between devices, on_device(): mid_rows = lax.all_gather(mid_low, 'tp', axis=0, tiled=True)  27.1 us
    all_gather x1, waiting for transfers between devices, on_device(): gathered_mlp = lax.all_gather(normed_mlp, 'tp', axis=0, tiled=True)  26.3 us
    reduce_scatter x1, waiting for transfers between devices, on_device(): lax.psum_scatter(jnp.dot(row_piece, out_weight, preferred_element_type=jn...  26.2 us
    all_gather x1, waiting for transfers between devices, on_device(): gathered_attn = lax.all_gather(normed_attn, 'tp', axis=0, tiled=True)  25.2 us
  transfers between devices with their start and end apart: 9, of which 8 were waited for; matrix products, arithmetic and copies ran while one was open for 8% of the time, Pallas kernels for 0%

commit v1 on v0

--- a/solution.py
+++ b/solution.py
@@ -211,15 +211,18 @@
         mlp_shift_grad,
         down_bias_grad,
     ) = lax.psum(
-        (
-            attn_gain_grad,
-            attn_shift_grad,
-            out_bias_grad,
-            mlp_gain_grad,
-            mlp_shift_grad,
-            down_bias_grad,
-        ),
-        ("dp", "tp"),
+        lax.psum(
+            (
+                attn_gain_grad,
+                attn_shift_grad,
+                out_bias_grad,
+                mlp_gain_grad,
+                mlp_shift_grad,
+                down_bias_grad,
+            ),
+            "tp",
+        ),
+        "dp",
     )
     return (
         layer_out,

time: 608 us -> 607 us (level)
  blocking collectives: 103 us -> 70.6 us
  waiting for transfers between devices: 329 us -> 361 us
    psum x1, blocking collectives: 39.3 us -> 7.1 us  [on_device(): lax.psum((attn_gain_grad, attn_shift_grad, out_bias_grad, mlp_gain_grad,...]
    psum x1, waiting for transfers between devices: 163 us -> 188 us  [on_device(): lax.psum((qkv_weight_grad, qv_bias_grad, out_weight_grad, up_weight_grad,...]
    reduce_scatter x1, waiting for transfers between devices: 0.01 us -> 7.63 us  [on_device(): lax.psum_scatter(jnp.einsum('te,de->td', row_piece, flat_qkv, preferred_e...]
  transfers between devices with their start and end apart: 9 -> 9, of which waited for: 8 -> 9; matrix products, arithmetic and copies ran while one was open for 8% -> 8% of each run, Pallas kernels for 0% -> 0%
where the time goes in v1:
time: 607 us; the launch traced here: 598 us
  waiting for transfers between devices  361 us (59%)
  matrix products  71.8 us (12%)
  blocking collectives  70.6 us (12%)
  local copies, waits for them, and re-layouts  44.1 us (7%)
  other arithmetic  34.8 us (6%)
  between operations  14.5 us (2%)
    psum x1, waiting for transfers between devices, on_device(): lax.psum((qkv_weight_grad, qv_bias_grad, out_weight_grad, up_weight_grad,...  188 us
    psum x1, blocking collectives, on_device(): lax.psum(lax.psum((attn_gain_grad, attn_shift_grad, out_bias_grad, mlp_ga...  63.5 us
    unnamed x83, local copies, waits for them, and re-layouts  34.2 us
    all_gather x1, waiting for transfers between devices, on_device(): mid_rows = lax.all_gather(mid_low, 'tp', axis=0, tiled=True)  27.1 us
    all_gather x1, waiting for transfers between devices, on_device(): gathered_mlp = lax.all_gather(normed_mlp, 'tp', axis=0, tiled=True)  26.3 us
    reduce_scatter x1, waiting for transfers between devices, on_device(): lax.psum_scatter(jnp.dot(row_piece, out_weight, preferred_element_type=jn...  26.2 us
    all_gather x1, waiting for transfers between devices, on_device(): gathered_attn = lax.all_gather(normed_attn, 'tp', axis=0, tiled=True)  25.2 us
    reduce_scatter x1, waiting for transfers between devices, on_device(): lax.psum_scatter(jnp.dot(row_piece, down_weight, preferred_element_type=j...  24.9 us
  transfers between devices with their start and end apart: 9, of which 9 were waited for; matrix products, arithmetic and copies ran while one was open for 8% of the time, Pallas kernels for 0%

profile of v1, /device:TPU:0, one launch (start us, length us, event | category | flops | bytes accessed | tf_op | source)
XLA Modules:
  0.0 598.5 jit_solution(3915339775010583106)
XLA Ops:
  13.0 3.8 copy.64
  17.5 25.2 %all-gather.5.cloned.1.call-done = bf16[1024,768]{1,0:T(8,128)(2,1)} async-done(((bf16[512,768]{1,0:T(8,128)(2,1)}), bf16[1024,768]{1,0:T(8,128)(2,1)}) %all-gather.5.cloned.1.call-update) | async-done | bytes 1572880 | tf_op jit(solution)/shard_map/all_gather | solution.py:59
  42.7 4.2 fusion.59
  66.3 26.2 %reduce-scatter.5.cloned.1.call-done = bf16[512,768]{1,0:T(8,128)(2,1)} async-done(((bf16[1024,768]{1,0:T(8,128)(2,1)}), bf16[512,768]{1,0:T(8,128)(2,1)}) %reduce-scatter.5.cloned.1.call-update) | async-done | bytes 786448 | tf_op jit(solution)/shard_map/reduce_scatter | solution.py:88
  98.1 26.3 %all-gather.7.cloned.1.call-done = bf16[1024,768]{1,0:T(8,128)(2,1)} async-done(((bf16[512,768]{1,0:T(8,128)(2,1)}), bf16[1024,768]{1,0:T(8,128)(2,1)}) %all-gather.7.cloned.1.call-update) | async-done | bytes 1572880 | tf_op jit(solution)/shard_map/all_gather | solution.py:96
  124.4 7.4 %fusion.60 = f32[1024,1536]{1,0:T(8,128)} fusion(bf16[1024,768]{1,0:T(8,128)(2,1)} %all-gather.7.cloned.1.call-done, bf16[768,1536]{1,0:T(8,128)(2,1)} %param.25), kind=kOutput, calls=%fused_computation.128 | convolution fusion | flops 2415919104 | bytes 10223616 | tf_op jit(solution)/shard_map/dot_general | solution.py:97
  131.8 21.3 %all-gather.9.cloned.1.call-done = bf16[1024,768]{1,0:T(8,128)(2,1)} async-done(((bf16[512,768]{1,0:T(8,128)(2,1)}), bf16[1024,768]{1,0:T(8,128)(2,1)}) %all-gather.9.cloned.1.call-update) | async-done | bytes 1572880 | tf_op jit(solution)/shard_map/all_gather | solution.py:108
  153.1 19.3 %convert_reduce_fusion = (f32[1536]{0:T(1024)S(1)}, bf16[1024,1536]{1,0:T(8,128)(2,1)S(1)}, f32[1024,1536]{1,0:T(8,128)}) fusion(f32[1024,1536]{1,0:T(8,128)} %fusion.60, f32[1536]{0:T(1024)S(1)} %copy-done.25, bf16[1024,768]{1,0:T(8,128)(2,1)} %all-gather.9.cloned.1.call-done, bf16[1536,768]{1,0:T(8,128)(2,1)S(1)} %copy-done), kind=kOutput, calls=%fused_computation.2 | convolution fusion | flops 2533882368 | bytes 19673088 | tf_op jit(solution)/shard_map/td,fd->tf/dot_general | solution.py:112
  174.1 3.8 convolution_convert_fusion.2
  178.0 6.2 %multiply_convert_fusion = bf16[1024,1536]{1,0:T(8,128)(2,1)S(1)} fusion(f32[1024,1536]{1,0:T(8,128)} %get-tuple-element.72, f32[1024,1536]{1,0:T(8,128)} %fusion.60, f32[1536]{0:T(1024)S(1)} %copy-done.25), kind=kLoop, calls=%fused_computation.4 | loop fusion | flops 6291456 | bytes 15734784 | tf_op jit(solution)/shard_map/convert_element_type | solution.py:98
  185.8 3.7 convolution_convert_fusion.3
  189.6 14.6 %reduce-scatter.9.cloned.1.call-done = bf16[512,768]{1,0:T(8,128)(2,1)} async-done(((bf16[1024,768]{1,0:T(8,128)(2,1)}), bf16[512,768]{1,0:T(8,128)(2,1)}) %reduce-scatter.9.cloned.1.call-update) | async-done | bytes 786448 | tf_op jit(solution)/shard_map/reduce_scatter | solution.py:120
  207.5 24.9 %reduce-scatter.7.cloned.1.call-done = bf16[512,768]{1,0:T(8,128)(2,1)} async-done(((bf16[1024,768]{1,0:T(8,128)(2,1)}), bf16[512,768]{1,0:T(8,128)(2,1)}) %reduce-scatter.7.cloned.1.call-update) | async-done | bytes 786448 | tf_op jit(solution)/shard_map/reduce_scatter | solution.py:100
  232.4 3.7 fusion.57
  238.5 27.1 %all-gather.11.cloned.1.call-done = bf16[1024,768]{1,0:T(8,128)(2,1)} async-done(((bf16[512,768]{1,0:T(8,128)(2,1)}), bf16[1024,768]{1,0:T(8,128)(2,1)}) %all-gather.11.cloned.1.call-update) | async-done | bytes 1572880 | tf_op jit(solution)/shard_map/all_gather | solution.py:134
  285.9 7.4 %fusion.62 = f32[1536,768]{1,0:T(8,128)} fusion(bf16[1024,1536]{1,0:T(8,128)(2,1)} %copy-done.8, bf16[1024,768]{1,0:T(8,128)(2,1)} %all-gather.9.cloned.1.call-done), kind=kOutput, calls=%fused_computation.130 | convolution fusion | flops 2415919104 | bytes 9437184 | tf_op jit(solution)/shard_map/tf,td->fd/dot_general | solution.py:109
  293.3 4.4 fusion.61
  300.2 3.8 fusion.63
  304.2 7.6 %reduce-scatter.11.cloned.1.call-done = bf16[512,768]{1,0:T(8,128)(2,1)} async-done(((bf16[1024,768]{1,0:T(8,128)(2,1)}), bf16[512,768]{1,0:T(8,128)(2,1)}) %reduce-scatter.11.cloned.1.call-update) | async-done | bytes 786448 | tf_op jit(solution)/shard_map/reduce_scatter | solution.py:177
  315.6 7.1 %all-reduce.2 = (f32[768]{0:T(1024)S(1)}, f32[768]{0:T(1024)S(1)}, f32[768]{0:T(1024)S(1)}, f32[768]{0:T(1024)S(1)}, f32[768]{0:T(1024)S(1)}, /*index=5*/f32[768]{0:T(1024)S(1)}) all-reduce(f32[768]{0:T(1024)S(1)} %get-tuple-element.44, f32[768]{0:T(1024)S(1)} %get-tuple-element.48, ...), channel_id=1, replica_groups=mesh['dp'=16,'tp'=2] {'tp'}, use_global_device_ids=true, to_apply=%region_18.19 | all-reduce | flops 4608 | bytes 36864 | tf_op jit(solution)/shard_map/psum | solution.py:214
  322.7 63.5 %all-reduce = (f32[768]{0:T(1024)}, f32[768]{0:T(1024)}, f32[2,384]{1,0:T(2,128)}, f32[768]{0:T(1024)}, f32[768]{0:T(1024)}, /*index=5*/f32[768]{0:T(1024)}, f32[1536]{0:T(1024)}, f32[768]{0:T(1024)}) all-reduce(f32[768]{0:T(1024)S(1)} %get-tuple-element.64, f32[768]{0:T(1024)S(1)} %get-tuple-element.65, ...), channel_id=1, replica_groups=mesh['dp'=16,'tp'=2] {'dp'}, use_global_device_ids=true, to_apply=%region_19.20 | all-reduce | flops 6912 | bytes 55296 | tf_op jit(solution)/shard_map/psum | solution.py:213
  389.3 187.6 %all-reduce.5.cloned.1.call-done = (f32[768,3,384]{0,2,1:T(8,128)}, f32[384,768]{1,0:T(8,128)}, f32[768,1536]{1,0:T(8,128)}, f32[1536,768]{1,0:T(8,128)}) async-done(((f32[768,3,384]{0,2,1:T(8,128)}, f32[384,768]{1,0:T(8,128)}, f32[768,1536]{1,0:T(8,128)}, f32[1536,768]{1,0:T(8,128)}), (f32[768,3,384]{0,2,1:T(8,128)}, f32[384,768]{1,0:T(8,128)}, f32[768,1536]{1,0:T(8,128)}, ...) | async-done | bytes 14155792 | tf_op jit(solution)/shard_map/psum | solution.py:195
  576.9 5.2 copy.87
  584.6 4.9 copy.147
  (155 shorter events, 74.9 us)
Async XLA Ops:
  7.2 145.9 %copy-start = (bf16[1536,768]{1,0:T(8,128)(2,1)S(1)}, bf16[1536,768]{1,0:T(8,128)(2,1)}, u32[]{:S(2)}) copy-start(bf16[1536,768]{1,0:T(8,128)(2,1)} %param.27) | copy-start | bytes 7077892
  7.2 5.5 copy-start.27
  7.2 35.5 %all-gather.5.cloned.1.call-start = ((), (), s32[]{:S(2)}) async-start(), calls=%async_computation.4 | async-start | bytes 2359296 | tf_op jit(solution)/shard_map/all_gather | solution.py:59
  12.6 79.8 %reduce-scatter.5.cloned.1.call-start = ((), (), s32[]{:S(2)}) async-start(), calls=%async_computation.5 | async-start | bytes 2359296 | tf_op jit(solution)/shard_map/reduce_scatter | solution.py:88
  64.0 28.4 %copy-start.1 = (bf16[512,768]{1,0:T(8,128)(2,1)S(1)}, bf16[512,768]{1,0:T(8,128)(2,1)}, u32[]{:S(2)}) copy-start(bf16[512,768]{1,0:T(8,128)(2,1)} %param.15) | copy-start | bytes 2359300
  64.0 28.4 %copy-start.22 = (f32[768]{0:T(1024)S(1)}, f32[768]{0:T(1024)}, u32[]{:S(2)}) copy-start(f32[768]{0:T(1024)} %param.22) | copy-start | bytes 9220
  66.2 29.4 %copy-start.24 = (f32[768]{0:T(1024)S(1)}, f32[768]{0:T(1024)}, u32[]{:S(2)}) copy-start(f32[768]{0:T(1024)} %param.23) | copy-start | bytes 9220
  66.2 29.4 %copy-start.26 = (f32[768]{0:T(1024)S(1)}, f32[768]{0:T(1024)}, u32[]{:S(2)}) copy-start(f32[768]{0:T(1024)} %param.24) | copy-start | bytes 9220
  66.2 58.1 %all-gather.7.cloned.1.call-start = ((), (), s32[]{:S(2)}) async-start(), calls=%async_computation.6 | async-start | bytes 2359296 | tf_op jit(solution)/shard_map/all_gather | solution.py:96
  97.0 56.1 %all-gather.9.cloned.1.call-start = ((), (), s32[]{:S(2)}) async-start(), calls=%async_computation.8 | async-start | bytes 2359296 | tf_op jit(solution)/shard_map/all_gather | solution.py:108
  97.6 55.5 %copy-start.25 = (f32[1536]{0:T(1024)S(1)}, f32[1536]{0:T(1024)}, u32[]{:S(2)}) copy-start(f32[1536]{0:T(1024)} %param.26) | copy-start | bytes 18436
  97.6 106.5 %reduce-scatter.9.cloned.1.call-start = ((), (), s32[]{:S(2)}) async-start(), calls=%async_computation.9 | async-start | bytes 2359296 | tf_op jit(solution)/shard_map/reduce_scatter | solution.py:120
  153.1 21.0 %copy-start.30 = (bf16[768,1536]{1,0:T(8,128)(2,1)S(1)}, bf16[768,1536]{1,0:T(8,128)(2,1)}, u32[]{:S(2)}) copy-start(bf16[768,1536]{1,0:T(8,128)(2,1)} %param.25) | copy-start | bytes 7077892
  177.9 54.4 %reduce-scatter.7.cloned.1.call-start = ((), (), s32[]{:S(2)}) async-start(), calls=%async_computation.7 | async-start | bytes 2359296 | tf_op jit(solution)/shard_map/reduce_scatter | solution.py:100
  189.5 42.8 %copy-start.28 = (f32[768]{0:T(1024)S(1)}, f32[768]{0:T(1024)}, u32[]{:S(2)}) copy-start(f32[768]{0:T(1024)} %param.28) | copy-start | bytes 9220
  189.5 76.1 %all-gather.11.cloned.1.call-start = ((), (), s32[]{:S(2)}) async-start(), calls=%async_computation.10 | async-start | bytes 2359296 | tf_op jit(solution)/shard_map/all_gather | solution.py:134
  238.3 73.6 %reduce-scatter.11.cloned.1.call-start = ((), (), s32[]{:S(2)}) async-start(), calls=%async_computation.11 | async-start | bytes 2359296 | tf_op jit(solution)/shard_map/reduce_scatter | solution.py:177
  285.6 291.3 %all-reduce.5.cloned.1.call-start = ((), (), s32[]{:S(2)}) async-start(), calls=%async_computation.12 | async-start | bytes 28311552 | tf_op jit(solution)/shard_map/psum | solution.py:195
  285.9 7.4 %copy-start.13 = (bf16[1024,1536]{1,0:T(8,128)(2,1)S(1)}, bf16[1024,1536]{1,0:T(8,128)(2,1)}, u32[]{:S(2)}) copy-start(bf16[1024,1536]{1,0:T(8,128)(2,1)} %copy-done.12) | copy-start | bytes 9437188
  285.9 7.4 %copy-start.17 = (bf16[1024,768]{1,0:T(8,128)(2,1)S(1)}, bf16[1024,768]{1,0:T(8,128)(2,1)}, u32[]{:S(2)}) copy-start(bf16[1024,768]{1,0:T(8,128)(2,1)} %all-gather.7.cloned.1.call-done) | copy-start | bytes 4718596
  293.3 4.4 copy-start.19
  304.0 7.8 %copy-start.23 = (f32[768]{0:T(1024)S(1)}, f32[768]{0:T(1024)}, u32[]{:S(2)}) copy-start(f32[768]{0:T(1024)} %param.17) | copy-start | bytes 9220
  582.1 7.4 %slice-start = ((s8[4718592]{0:T(1024)(128)(4,1)}), s8[4194304]{0:T(1024)(128)(4,1)S(1)}, s32[]{:S(2)}) async-start(s8[4718592]{0:T(1024)(128)(4,1)} %bitcast.79), calls=%async_computation.13 | async-start | bytes 8388608
  584.6 4.9 slice-start.1
  (21 other events, 43.7 us)
Sparse Core Ops, SparseCore 0:
  12.8 29.8 all-gather.4
  66.3 26.0 reduce-scatter.4
  97.1 27.2 all-gather.6
  125.8 27.2 all-gather.8
  178.0 26.0 reduce-scatter.8
  206.2 26.0 reduce-scatter.6
  238.4 27.2 all-gather.10
  285.7 26.0 reduce-scatter.10
  317.6 259.3 all-reduce.4
